TPU v7x, 512 devices: a whole 4x8x8 slice. The times are simulated.
512 devices in a mesh: aux: 8 (over z), ao: 16 (over y, core), orb: 4 (over x).
Axes of the slice: x: 4, y: 8, z: 8, core: 2. Of those that a mesh axis runs over, the one named last changes fastest.
Arguments:
- integrals: bfloat16 [128, 16, 4, 128, 128], P('aux', 'ao', None, 'orb'), may hold values from -6 to 6
- partner: int32 [16, 4], P('ao'), may hold values from 0 to 15
- pair_count: int32 [16], P('ao'), may hold values from 1 to 4
- occupied_coeff: bfloat16 [2048, 512], P('ao', 'orb'), may hold values from -0.25 to 0.25
- occupied_domain: int32 [16, 4], P('ao', 'orb'), may hold values 0 or 1
- virtual_coeff: bfloat16 [2048, 8192], P('aux', 'ao'), may hold values from -0.125 to 0.125
- virtual_domain: int32 [16, 64], P(None, 'ao'), may hold values 0 or 1
Outputs:
- transformed: bfloat16 [128, 512, 8192], P('aux', 'orb', 'ao')
All inputs are finite; a program needn't handle non-finite values. No bound on the sum of `occupied_domain` or of `virtual_domain` on one device may be relied on, other than what follows from the above.
Results may differ from a plain program's by a relative error of at most 0.0049.
Values may be sent and summed in bfloat16 or wider, within the bound.
A program may use at most 64 MiB of HBM per device.

v0:
```python
import jax
import jax.numpy as jnp
from jax import lax
from jax.sharding import PartitionSpec as P


def local(
    integrals, partner, pair_count, occupied_coeff, occupied_domain, virtual_coeff, virtual_domain
):
    block_size = integrals.shape[4]
    slab_rows = integrals.shape[0]
    local_blocks = integrals.shape[1]
    slot_count = integrals.shape[2]
    occ_width = occupied_coeff.shape[1]
    domain_wire = occupied_domain.astype(jnp.bfloat16)
    all_occ, all_domain = (
        lax.all_gather(occupied_coeff, "ao", axis=0, tiled=True),
        lax.all_gather(domain_wire, "ao", axis=0, tiled=True),
    )
    occ_mask = jnp.repeat(jnp.repeat(all_domain, block_size, axis=0), block_size, axis=1)
    occ_masked = all_occ * occ_mask
    block_total = all_domain.shape[0]
    picked = occ_masked.reshape(block_total, block_size, occ_width)[partner]
    slots = jnp.arange(slot_count, dtype=jnp.int32)
    live = (slots[None, :] < pair_count[:, None]).astype(jnp.bfloat16)
    picked = picked * live[:, :, None, None]
    all_columns = lax.all_to_all(picked, "orb", split_axis=2, concat_axis=3, tiled=True)
    partial_term = jnp.einsum(
        "nkri,pnkrv->pinv", all_columns, integrals, preferred_element_type=jnp.float32
    )
    half_wide = lax.psum_scatter(partial_term, "orb", scatter_dimension=1, tiled=True)
    half_local = half_wide.reshape(slab_rows, occ_width, local_blocks * block_size).astype(
        jnp.bfloat16
    )
    vir_rows = lax.all_gather(virtual_coeff, "aux", axis=0, tiled=True)
    vir_mask = jnp.repeat(
        jnp.repeat(virtual_domain, block_size, axis=0), block_size, axis=1
    ).astype(jnp.bfloat16)
    vir_masked = vir_rows * vir_mask
    vir_width = vir_masked.shape[1]
    piece = lax.all_gather(half_local, "ao", axis=2, tiled=True)
    count = piece.shape[2]
    flat = piece.reshape(slab_rows * occ_width, count)
    product = jnp.dot(flat, vir_masked, preferred_element_type=jnp.float32)
    result = product.reshape(slab_rows, occ_width, vir_width)
    return result.astype(jnp.bfloat16)


def solution(mesh):
    placed = (
        P("aux", "ao", None, "orb", None),
        P("ao", None),
        P("ao"),
        P("ao", "orb"),
        P("ao", "orb"),
        P("aux", "ao"),
        P(None, "ao"),
    )
    return jax.shard_map(
        local, mesh=mesh, in_specs=placed, out_specs=P("aux", "orb", "ao"), check_vma=False
    )
```

profile of v0, /device:TPU:1, one launch (start us, length us, event | category | flops | bytes accessed | tf_op | source)
XLA Modules:
  0.0 215.5 jit_solution(4892264346600140509)
XLA Ops:
  7.4 0.0 copy-start
  7.4 0.0 reduce-scatter.2.cloned.1.call-start
  8.7 0.7 fusion.11
  9.4 1.3 dynamic-slice
  10.7 0.7 dynamic-update-slice
  11.3 29.8 %all-reduce = bf16[16]{0:T(256)(128)(2,1)S(1)} all-reduce(bf16[16]{0:T(256)(128)(2,1)S(1)} %dynamic-update-slice), channel_id=1, replica_groups=mesh['aux'=8,'ao'=16,'orb'=4] {'ao'}, use_global_device_ids=true, to_apply=%add | all-reduce | flops 16 | bytes 64
  41.1 0.1 broadcast_bitcast_fusion
  41.2 16.4 %all_gather.14 = bf16[2048,128]{1,0:T(8,128)(2,1)S(1)} all-gather(bf16[128,128]{1,0:T(8,128)(2,1)} %param.10), channel_id=1, replica_groups=mesh['aux'=8,'ao'=16,'orb'=4] {'ao'}, dimensions={0}, use_global_device_ids=true | all-gather | bytes 557056 | tf_op jit(solution)/shard_map/all_gather | solution.py:17
  57.6 0.3 broadcast_multiply_fusion
  58.0 0.6 gather_fusion
  58.5 0.1 bitcast_multiply_fusion.1
  58.6 0.1 copy.14
  58.7 7.3 %all_to_all.15 = bf16[1,4,128,128]{3,1,0,2:T(4,128)(2,1)S(1)} all-to-all(bf16[1,4,128,128]{3,1,0,2:T(4,128)(2,1)S(1)} %copy.14), channel_id=1, replica_groups=mesh['aux'=8,'ao'=16,'orb'=4] {'orb'}, dimensions={2} | all-to-all | bytes 262144 | tf_op jit(solution)/shard_map/all_to_all | solution.py:27
  66.1 0.1 copy.16
  66.1 0.1 reshape.70
  66.2 0.0 copy-done
  66.2 2.7 %convolution_bitcast_fusion = f32[16,512,1,128]{3,1,0,2:T(8,128)} fusion(bf16[4,32,512,1]{2,1,0,3:T(8,128)(2,1)S(1)} %reshape.70, bf16[16,1,4,32,128]{4,3,2,1,0:T(8,128)(2,1)S(1)} %copy-done), kind=kOutput, calls=%fused_computation.3 | convolution fusion | flops 268435456 | bytes 4849664 | tf_op jit(solution)/shard_map/nkri,pnkrv->pinv/dot_general | solution.py:28
  68.9 0.0 reduce-scatter.2.cloned.1.call-update
  68.9 0.0 copy-start.1
  68.9 0.0 all-gather.4.cloned.1.call-start
  69.0 0.5 all-gather.4.cloned.1.call-update
  69.5 0.0 all-gather.6.cloned.1.call-start
  69.6 51.7 %reduce-scatter.2.cloned.1.call-done = f32[16,128,1,128]{3,1,0,2:T(8,128)} async-done(((f32[16,512,1,128]{3,1,0,2:T(8,128)}), f32[16,128,1,128]{3,1,0,2:T(8,128)}) %reduce-scatter.2.cloned.1.call-update) | async-done | bytes 1048592 | tf_op jit(solution)/shard_map/reduce_scatter | solution.py:31
  121.2 2.1 convert_element_type.34
  123.3 0.0 all-gather.6.cloned.1.call-update
  123.4 0.0 copy-done.1
  123.4 0.1 copy.17
  123.5 0.0 all-gather.4.cloned.1.call-done
  123.5 0.0 copy-start.2
  123.5 69.4 %all-gather.6.cloned.1.call-done = bf16[16,128,1,2048]{3,1,0,2:T(8,128)(2,1)} async-done(((bf16[16,128,1,128]{3,1,0,2:T(8,128)(2,1)}), bf16[16,128,1,2048]{3,1,0,2:T(8,128)(2,1)}) %all-gather.6.cloned.1.call-update) | async-done | bytes 8388624 | tf_op jit(solution)/shard_map/all_gather | solution.py:41
  192.9 0.1 broadcast_in_dim.21
  193.0 5.8 %broadcast_in_dim.22 = bf16[2048,4,128]{2,1,0:T(4,128)(2,1)S(1)} broadcast(bf16[2048,4]{1,0:T(8,128)(2,1)S(1)} %bitcast.47), dimensions={0,1} | broadcast | bytes 2113536 | tf_op jit(solution)/shard_map/broadcast_in_dim | solution.py:36
  198.7 0.0 copy-done.2
  198.8 9.3 %fusion.5 = bf16[16,128,512]{2,1,0:T(8,128)(2,1)} fusion(bf16[2048,512]{1,0:T(8,128)(2,1)S(1)} %copy-done.2, bf16[256,8,4,128]{3,2,1,0:T(4,128)(2,1)S(1)} %bitcast.46, bf16[16,128,1,2048]{3,1,0,2:T(8,128)(2,1)} %all-gather.6.cloned.1.call-done), kind=kOutput, calls=%fused_computation.7 | convolution fusion | flops 4297064448 | bytes 14680064 | tf_op jit(solution)/shard_map/dot_general | solution.py:44
  (5 shorter events, 0.0 us)
Async XLA Ops:
  7.4 58.8 %copy-start = (bf16[16,1,4,32,128]{4,3,2,1,0:T(8,128)(2,1)S(1)}, bf16[16,1,4,32,128]{4,3,2,1,0:T(8,128)(2,1)}, u32[]{:S(2)}) copy-start(bf16[16,1,4,32,128]{4,3,2,1,0:T(8,128)(2,1)} %param.7) | copy-start | bytes 1572868
  7.4 113.9 %reduce-scatter.2.cloned.1.call-start = ((), (), s32[]{:S(2)}) async-start(), calls=%async_computation.2 | async-start | bytes 5242880 | tf_op jit(solution)/shard_map/reduce_scatter | solution.py:31
  68.9 54.5 %copy-start.1 = (s32[16,4]{0,1:T(4,128)S(1)}, s32[16,4]{0,1:T(4,128)}, u32[]{:S(2)}) copy-start(s32[16,4]{0,1:T(4,128)} %param.13) | copy-start | bytes 772
  68.9 54.6 %all-gather.4.cloned.1.call-start = ((), (), s32[]{:S(2)}) async-start(), calls=%async_computation.3 | async-start | bytes 2359296 | tf_op jit(solution)/shard_map/all_gather | solution.py:35
  69.5 123.4 %all-gather.6.cloned.1.call-start = ((), (), s32[]{:S(2)}) async-start(), calls=%async_computation.4 | async-start | bytes 8912896 | tf_op jit(solution)/shard_map/all_gather | solution.py:41
  123.5 75.3 %copy-start.2 = (bf16[2048,512]{1,0:T(8,128)(2,1)S(1)}, bf16[2048,512]{1,0:T(8,128)(2,1)}, u32[]{:S(2)}) copy-start(bf16[2048,512]{1,0:T(8,128)(2,1)} %all-gather.4.cloned.1.call-done) | copy-start | bytes 6291460
Sparse Core Ops, SparseCore 0:
  69.0 52.1 reduce-scatter.1
Sparse Core Ops, SparseCore 1:
  71.5 40.2 all-gather.3
  123.5 69.4 all-gather.5
where the time goes:
time: 216 us
  waiting for transfers between devices  122 us (56%)
  blocking collectives  53.5 us (25%)
  between operations  16.3 us (8%)
  matrix products  12 us (6%)
  local copies, waits for them, and re-layouts  8.79 us (4%)
  other arithmetic  3.2 us (1%)
    all_gather x1, waiting for transfers between devices, local(): piece = lax.all_gather(half_local, 'ao', axis=2, tiled=True)  69.4 us
    reduce_scatter x1, waiting for transfers between devices, local(): lax.psum_scatter(partial_term, 'orb', scatter_dimension=1, tiled=True)  51.7 us
    unnamed x1, blocking collectives  29.8 us
    all_gather x1, blocking collectives, local(): lax.all_gather(occupied_coeff, 'ao', axis=0, tiled=True)  16.4 us
    dot_general x1, matrix products, local(): product = jnp.dot(flat, vir_masked, preferred_element_type=jnp.float32)  9.32 us
    all_to_all x1, blocking collectives, local(): lax.all_to_all(picked, 'orb', split_axis=2, concat_axis=3, tiled=True)  7.31 us
    broadcast_in_dim x1, local copies, waits for them, and re-layouts, local(): jnp.repeat(jnp.repeat(virtual_domain, block_size, axis=0), block_size, ax...  5.78 us
  transfers between devices with their start and end apart: 3, of which 2 were waited for; matrix products, arithmetic and copies ran while one was open for 1% of the time, Pallas kernels for 0%

commit v1 on v0

--- a/solution.py
+++ b/solution.py
@@ -24,7 +24,10 @@
     slots = jnp.arange(slot_count, dtype=jnp.int32)
     live = (slots[None, :] < pair_count[:, None]).astype(jnp.bfloat16)
     picked = picked * live[:, :, None, None]
-    all_columns = lax.all_to_all(picked, "orb", split_axis=2, concat_axis=3, tiled=True)
+    all_columns = jnp.concatenate(
+        lax.all_to_all(jnp.stack(jnp.split(picked, lax.axis_size("orb"), axis=2)), "orb", 0, 0),
+        axis=3,
+    )
     partial_term = jnp.einsum(
         "nkri,pnkrv->pinv", all_columns, integrals, preferred_element_type=jnp.float32
     )

time: 216 us -> 216 us (level)
  no operation moved by 1% of the time
where the time goes in v1:
time: 216 us
  waiting for transfers between devices  122 us (56%)
  blocking collectives  53.5 us (25%)
  between operations  16.3 us (8%)
  matrix products  12 us (6%)
  local copies, waits for them, and re-layouts  8.91 us (4%)
  other arithmetic  3.22 us (1%)
    all_gather x1, waiting for transfers between devices, local(): piece = lax.all_gather(half_local, 'ao', axis=2, tiled=True)  69.4 us
    reduce_scatter x1, waiting for transfers between devices, local(): lax.psum_scatter(partial_term, 'orb', scatter_dimension=1, tiled=True)  51.7 us
    unnamed x1, blocking collectives  29.8 us
    all_gather x1, blocking collectives, local(): lax.all_gather(occupied_coeff, 'ao', axis=0, tiled=True)  16.4 us
    dot_general x1, matrix products, local(): product = jnp.dot(flat, vir_masked, preferred_element_type=jnp.float32)  9.32 us
    all_to_all x1, blocking collectives, local(): lax.all_to_all(jnp.stack(jnp.split(picked, lax.axis_size('orb'), axis=2))...  7.31 us
    broadcast_in_dim x1, local copies, waits for them, and re-layouts, local(): jnp.repeat(jnp.repeat(virtual_domain, block_size, axis=0), block_size, ax...  5.78 us
  transfers between devices with their start and end apart: 3, of which 2 were waited for; matrix products, arithmetic and copies ran while one was open for 1% of the time, Pallas kernels for 0%

profile of v1, /device:TPU:1, one launch (start us, length us, event | category | flops | bytes accessed | tf_op | source)
XLA Modules:
  0.0 215.6 jit_solution(4295837192295602892)
XLA Ops:
  7.4 0.0 copy-start
  7.4 0.0 reduce-scatter.2.cloned.1.call-start
  8.7 0.7 fusion.11
  9.4 1.3 dynamic-slice
  10.7 0.8 dynamic-update-slice
  11.5 29.8 %all-reduce = bf16[16]{0:T(256)(128)(2,1)S(1)} all-reduce(bf16[16]{0:T(256)(128)(2,1)S(1)} %dynamic-update-slice), channel_id=1, replica_groups=mesh['aux'=8,'ao'=16,'orb'=4] {'ao'}, use_global_device_ids=true, to_apply=%add | all-reduce | flops 16 | bytes 64
  41.3 0.1 broadcast_bitcast_fusion
  41.4 16.4 %all_gather.14 = bf16[2048,128]{1,0:T(8,128)(2,1)S(1)} all-gather(bf16[128,128]{1,0:T(8,128)(2,1)} %param.10), channel_id=1, replica_groups=mesh['aux'=8,'ao'=16,'orb'=4] {'ao'}, dimensions={0}, use_global_device_ids=true | all-gather | bytes 557056 | tf_op jit(solution)/shard_map/all_gather | solution.py:17
  57.8 0.3 broadcast_multiply_fusion
  58.2 0.6 gather_fusion
  58.7 0.1 bitcast_multiply_fusion.1
  58.9 7.3 %all_to_all.5 = bf16[4,1,4,32,128]{4,3,2,1,0:T(8,128)(2,1)S(1)} all-to-all(bf16[4,1,4,32,128]{4,3,2,1,0:T(8,128)(2,1)S(1)} %pad_maximum_fusion), channel_id=1, replica_groups=mesh['aux'=8,'ao'=16,'orb'=4] {'orb'}, dimensions={0} | all-to-all | bytes 262144 | tf_op jit(solution)/shard_map/all_to_all | solution.py:28
  66.2 0.1 copy.12
  66.3 0.1 reshape.75
  66.3 0.0 copy-done
  66.4 2.7 %convolution_bitcast_fusion = f32[16,512,1,128]{3,1,0,2:T(8,128)} fusion(bf16[4,32,512,1]{2,1,0,3:T(8,128)(2,1)S(1)} %reshape.75, bf16[16,1,4,32,128]{4,3,2,1,0:T(8,128)(2,1)S(1)} %copy-done), kind=kOutput, calls=%fused_computation.3 | convolution fusion | flops 268435456 | bytes 4849664 | tf_op jit(solution)/shard_map/nkri,pnkrv->pinv/dot_general | solution.py:31
  69.0 0.0 reduce-scatter.2.cloned.1.call-update
  69.1 0.0 copy-start.1
  69.1 0.0 all-gather.4.cloned.1.call-start
  69.1 0.5 all-gather.4.cloned.1.call-update
  69.7 0.0 all-gather.6.cloned.1.call-start
  69.7 51.7 %reduce-scatter.2.cloned.1.call-done = f32[16,128,1,128]{3,1,0,2:T(8,128)} async-done(((f32[16,512,1,128]{3,1,0,2:T(8,128)}), f32[16,128,1,128]{3,1,0,2:T(8,128)}) %reduce-scatter.2.cloned.1.call-update) | async-done | bytes 1048592 | tf_op jit(solution)/shard_map/reduce_scatter | solution.py:34
  121.4 2.1 convert_element_type.34
  123.5 0.0 all-gather.6.cloned.1.call-update
  123.5 0.0 copy-done.1
  123.5 0.1 copy.13
  123.6 0.0 all-gather.4.cloned.1.call-done
  123.6 0.0 copy-start.2
  123.6 69.4 %all-gather.6.cloned.1.call-done = bf16[16,128,1,2048]{3,1,0,2:T(8,128)(2,1)} async-done(((bf16[16,128,1,128]{3,1,0,2:T(8,128)(2,1)}), bf16[16,128,1,2048]{3,1,0,2:T(8,128)(2,1)}) %all-gather.6.cloned.1.call-update) | async-done | bytes 8388624 | tf_op jit(solution)/shard_map/all_gather | solution.py:44
  193.0 0.1 broadcast_in_dim.21
  193.1 5.8 %broadcast_in_dim.22 = bf16[2048,4,128]{2,1,0:T(4,128)(2,1)S(1)} broadcast(bf16[2048,4]{1,0:T(8,128)(2,1)S(1)} %bitcast.53), dimensions={0,1} | broadcast | bytes 2113536 | tf_op jit(solution)/shard_map/broadcast_in_dim | solution.py:39
  198.9 0.0 copy-done.2
  198.9 9.3 %fusion.5 = bf16[16,128,512]{2,1,0:T(8,128)(2,1)} fusion(bf16[2048,512]{1,0:T(8,128)(2,1)S(1)} %copy-done.2, bf16[256,8,4,128]{3,2,1,0:T(4,128)(2,1)S(1)} %bitcast.52, bf16[16,128,1,2048]{3,1,0,2:T(8,128)(2,1)} %all-gather.6.cloned.1.call-done), kind=kOutput, calls=%fused_computation.7 | convolution fusion | flops 4297064448 | bytes 14680064 | tf_op jit(solution)/shard_map/dot_general | solution.py:47
  (6 shorter events, 0.0 us)
Async XLA Ops:
  7.4 59.0 %copy-start = (bf16[16,1,4,32,128]{4,3,2,1,0:T(8,128)(2,1)S(1)}, bf16[16,1,4,32,128]{4,3,2,1,0:T(8,128)(2,1)}, u32[]{:S(2)}) copy-start(bf16[16,1,4,32,128]{4,3,2,1,0:T(8,128)(2,1)} %param.7) | copy-start | bytes 1572868
  7.4 114.0 %reduce-scatter.2.cloned.1.call-start = ((), (), s32[]{:S(2)}) async-start(), calls=%async_computation.2 | async-start | bytes 5242880 | tf_op jit(solution)/shard_map/reduce_scatter | solution.py:34
  69.1 54.5 %copy-start.1 = (s32[16,4]{0,1:T(4,128)S(1)}, s32[16,4]{0,1:T(4,128)}, u32[]{:S(2)}) copy-start(s32[16,4]{0,1:T(4,128)} %param.13) | copy-start | bytes 772
  69.1 54.6 %all-gather.4.cloned.1.call-start = ((), (), s32[]{:S(2)}) async-start(), calls=%async_computation.3 | async-start | bytes 2359296 | tf_op jit(solution)/shard_map/all_gather | solution.py:38
  69.7 123.4 %all-gather.6.cloned.1.call-start = ((), (), s32[]{:S(2)}) async-start(), calls=%async_computation.4 | async-start | bytes 8912896 | tf_op jit(solution)/shard_map/all_gather | solution.py:44
  123.6 75.3 %copy-start.2 = (bf16[2048,512]{1,0:T(8,128)(2,1)S(1)}, bf16[2048,512]{1,0:T(8,128)(2,1)}, u32[]{:S(2)}) copy-start(bf16[2048,512]{1,0:T(8,128)(2,1)} %all-gather.4.cloned.1.call-done) | copy-start | bytes 6291460
Sparse Core Ops, SparseCore 0:
  69.2 52.1 reduce-scatter.1
Sparse Core Ops, SparseCore 1:
  71.6 40.1 all-gather.3
  123.6 69.4 all-gather.5
